TPU v7x, 32 devices: a whole 2x2x4 slice. The times are simulated.
32 devices in a mesh: groups: 2 (over y), tm: 16 (over z, x, core).
Axes of the slice: x: 2, y: 2, z: 4, core: 2. Of those that a mesh axis runs over, the one named last changes fastest.
Arguments:
- frames: bfloat16 [4096, 8192], P('tm', 'groups'), parts along dimension 1, may hold values from -6 to 6
- frame_valid: int32 [8192], P(('groups', 'tm')), parts along dimension 0, may hold values 0 or 1
- valid_count: int32 [32], P('groups'), parts along dimension 0, may hold values from 32 to 128, as said below
- block_map: int32 [32, 256], P('groups'), parts along dimension 0, may hold values from 0 to 255, as said below
- offsets: int32 [4, 2], replicated, may hold values from -4 to 4
Outputs:
- cross: float32 [512, 4, 2, 2048], P(('groups', 'tm')), parts along dimension 0
There are 2 independent parts, one for each index of `groups`. A program takes and returns all parts, laid end to end along the dimension named above; an argument that names none is the same for every part. Nothing has to cross between parts.
Inputs may be any that keep to these rules, and one draw needn't show every extreme that they name: `valid_count`: at most half of a tile's pixels are valid. Some tile has exactly 128 valid pixels and another exactly 32 in every draw; the others are spread evenly between the two. `block_map`: each row is a permutation of the pixels of a tile. Row steps lie in -4 to 4.
All inputs are finite; a program needn't handle non-finite values. No bound on the sum of `frame_valid` on one device may be relied on, other than what follows from the above.
Results may differ from a plain program's by a relative error of at most 0.0052.
Values may be sent and summed in bfloat16 or wider, within the bound.
No kernel may reach another device: no remote copies, remote signals or barrier semaphores. Data moves between devices by JAX's collectives and lax.ppermute only.
A program may use at most 64 MiB of HBM per device.

v0:
```python
import math
import jax
import jax.numpy as jnp
from jax import lax
from jax.sharding import PartitionSpec as P

ROWS = 16
BAND = 256
REACH = 4


def base_angles(frames_len, band_width):
    frame_idx = jnp.arange(frames_len, dtype=jnp.int32)[:, None]
    bin_idx = jnp.arange(band_width, dtype=jnp.int32)[None, :]
    angles = (frame_idx * bin_idx % frames_len).astype(jnp.float32) * (2.0 * math.pi / frames_len)
    return (jnp.cos(angles), jnp.sin(angles))


def rotated_table(base_cos, base_sin, bin_start):
    frames_len = base_cos.shape[0]
    frame_idx = jnp.arange(frames_len, dtype=jnp.int32)
    phase = (frame_idx * bin_start % frames_len).astype(jnp.float32) * (2.0 * math.pi / frames_len)
    phase_cos = jnp.cos(phase)[:, None]
    phase_sin = jnp.sin(phase)[:, None]
    scaling = 1.0 / math.sqrt(frames_len)
    real_part = base_cos * phase_cos - base_sin * phase_sin
    imag_part = -(base_sin * phase_cos + base_cos * phase_sin)
    return (jnp.concatenate([real_part, imag_part], axis=1) * scaling).astype(jnp.bfloat16)


def nearby_validity(valid_count, block_map, position):
    tile_pix = block_map.shape[1]
    padded_count = jnp.pad(valid_count, ((1, 1),))
    padded_map = jnp.pad(block_map, ((1, 1), (0, 0)))
    counts = lax.dynamic_slice_in_dim(padded_count, position, 3, 0)
    slots_map = lax.dynamic_slice_in_dim(padded_map, position, 3, 0)
    slot_idx = jnp.arange(tile_pix, dtype=jnp.int32)
    live = (slot_idx[None, :] < counts[:, None]).astype(jnp.float32)
    match = (slots_map[:, :, None] == slot_idx[None, None, :]).astype(jnp.float32)
    return jnp.sum(live[:, :, None] * match, axis=1)


def transform(columns, table):
    return lax.dot_general(
        columns, table, (((0,), (0,)), ((), ())), preferred_element_type=jnp.float32
    )


def cross_block(extended, ext_valid, offsets, tile_width):
    spectra = extended.astype(jnp.float32)
    row_count = spectra.shape[0]
    half = spectra.shape[2] // 2
    padded = jnp.pad(spectra, ((REACH, REACH), (0, 0), (0, 0)))
    padded_valid = jnp.pad(ext_valid, ((REACH, REACH), (0, 0)))
    own_spec = spectra[:, REACH : REACH + tile_width]
    own_valid = ext_valid[:, REACH : REACH + tile_width]
    own_real = own_spec[..., :half]
    own_imag = own_spec[..., half:]
    results = []
    for which in range(offsets.shape[0]):
        row_step = offsets[which, 0] + REACH
        col_step = offsets[which, 1] + REACH
        shifted = lax.dynamic_slice(
            padded, (row_step, col_step, jnp.int32(0)), (row_count, tile_width, 2 * half)
        )
        shifted_valid = lax.dynamic_slice(
            padded_valid, (row_step, col_step), (row_count, tile_width)
        )
        other_real = shifted[..., :half]
        other_imag = shifted[..., half:]
        real_part = jnp.sum(own_real * other_real + own_imag * other_imag, axis=0)
        imag_part = jnp.sum(own_imag * other_real - own_real * other_imag, axis=0)
        pair_count = jnp.sum(own_valid * shifted_valid, axis=0)
        scaling = 1.0 / jnp.maximum(pair_count, 1.0)
        results.append(jnp.stack([real_part, imag_part], axis=1) * scaling[:, None, None])
    return jnp.stack(results, axis=1)


def per_device(frames, frame_valid, valid_count, block_map, offsets):
    tile_count = lax.axis_size("tm")
    position = lax.axis_index("tm")
    frame_dev, pixel_count = frames.shape
    tile_pix = pixel_count // tile_count
    tile_width = tile_pix // ROWS
    masked = frames * frame_valid[:, None].astype(jnp.bfloat16)
    grouped = masked.reshape(frame_dev, tile_count, tile_pix)
    nearby = nearby_validity(valid_count, block_map, position).reshape(3, ROWS, tile_width)
    ext_valid = jnp.concatenate(
        [nearby[0][:, tile_width - REACH :], nearby[1], nearby[2][:, :REACH]], axis=1
    )
    own_valid = nearby[1].reshape(tile_pix)
    tiled = grouped.reshape(frame_dev, tile_count, ROWS, tile_width)
    blank = jnp.zeros((frame_dev, 1, ROWS, REACH), jnp.bfloat16)
    left_side = jnp.concatenate([blank, tiled[:, :-1, :, tile_width - REACH :]], axis=1)
    right_side = jnp.concatenate([tiled[:, 1:, :, :REACH], blank], axis=1)
    margins = jnp.concatenate([left_side, right_side], axis=3).reshape(
        frame_dev, tile_count, ROWS * 2 * REACH
    )
    tile_frames, margin_frames = (
        lax.all_to_all(grouped, "tm", split_axis=1, concat_axis=0, tiled=True),
        lax.all_to_all(margins, "tm", split_axis=1, concat_axis=0, tiled=True),
    )
    margin_frames = margin_frames.reshape(-1, ROWS * 2 * REACH)
    margin_valid = jnp.concatenate(
        [ext_valid[:, :REACH], ext_valid[:, REACH + tile_width :]], axis=1
    ).reshape(-1)
    tile_frames = tile_frames.reshape(-1, tile_pix)
    frames_len = tile_frames.shape[0]
    bins = frames_len // 2
    base_cos, base_sin = base_angles(frames_len, BAND)

    def own_spectra(table):
        spectra = transform(tile_frames, table) * own_valid[:, None]
        return spectra.astype(jnp.bfloat16).reshape(ROWS, tile_width, table.shape[1])

    def one_band(band_index, result):
        bin_start = (band_index * BAND).astype(jnp.int32)
        table = rotated_table(base_cos, base_sin, bin_start)
        own_spec = own_spectra(table)
        edge_spec = (transform(margin_frames, table) * margin_valid[:, None]).astype(jnp.bfloat16)
        edge_spec = edge_spec.reshape(ROWS, 2 * REACH, table.shape[1])
        extended = jnp.concatenate([edge_spec[:, :REACH], own_spec, edge_spec[:, REACH:]], axis=1)
        band_cross = cross_block(extended, ext_valid, offsets, tile_width)
        return lax.dynamic_update_slice(
            result, band_cross, (jnp.int32(0), jnp.int32(0), jnp.int32(0), bin_start)
        )

    result = jnp.zeros((tile_width, offsets.shape[0], 2, bins), jnp.float32)
    return lax.fori_loop(0, bins // BAND, one_band, result)


def solution(mesh):
    return jax.shard_map(
        per_device,
        mesh=mesh,
        in_specs=(P("tm", "groups"), P(("groups", "tm")), P("groups"), P("groups", None), P()),
        out_specs=P(("groups", "tm"), None, None, None),
        check_vma=False,
    )
```

profile of v0, /device:TPU:11, one launch (start us, length us, event | category | flops | bytes accessed | tf_op | source)
XLA Modules:
  0.0 280.0 jit_solution(15077811135383140968)
XLA Ops:
  0.0 3.3 %copy.13 = bf16[256,4096]{0,1:T(8,128)(2,1)S(1)} copy(bf16[256,4096]{1,0:T(8,128)(2,1)} %param.7) | data formatting | bytes 4194304 | tf_op args[0]
  3.3 1.5 broadcast_multiply_fusion
  4.8 2.0 fusion.44
  6.9 0.7 fusion.41
  7.5 31.1 %all_to_all.30 = bf16[256,16,128]{0,2,1:T(8,128)(2,1)S(1)} all-to-all(bf16[256,16,128]{0,2,1:T(8,128)(2,1)S(1)} %fusion.41), channel_id=1, replica_groups=mesh['groups'=2,'tm'=16] {'tm'}, dimensions={1} | all-to-all | bytes 2097152 | tf_op jit(solution)/shard_map/all_to_all | solution.py:101
  38.6 4.9 %all-to-all-start.1 = ((bf16[256,16,256]{0,2,1:T(8,128)(2,1)}), bf16[256,16,256]{0,2,1:T(8,128)(2,1)S(1)}, u32[]{:S(2)}, u32[]{:S(2)}) async-start(bf16[256,16,256]{0,2,1:T(8,128)(2,1)} %bitcast.5), calls=%async_computation.1 | async-start | bytes 4194304 | tf_op jit(solution)/shard_map/all_to_all | solution.py:100
  43.6 0.7 fusion.45
  55.4 1.3 copy.14
  56.7 34.2 %all-to-all-done.1 = bf16[256,16,256]{0,2,1:T(8,128)(2,1)S(1)} async-done(((bf16[256,16,256]{0,2,1:T(8,128)(2,1)}), bf16[256,16,256]{0,2,1:T(8,128)(2,1)S(1)}, u32[]{:S(2)}, u32[]{:S(2)}) %all-to-all-start.1) | async-done | bytes 2097184 | tf_op jit(solution)/shard_map/all_to_all | solution.py:100
  91.0 2.4 copy.15
  93.3 0.5 broadcast_in_dim.14
  93.9 185.2 %while.19 = (s32[]{:T(128)}, f32[16,4,2,2048]{3,2,1,0:T(2,128)S(1)}, bf16[4096,128]{1,0:T(8,128)(2,1)}, f32[16,8]{1,0:T(8,128)}, bf16[4096,256]{1,0:T(8,128)(2,1...) while((s32[]{:T(128)}, ...), condition=%wide.wide.region_14.15_spmd.clone.clone, body=%wide.wide.region_1.14_spmd.clone.clone.sunk | while | flops 1649076224 | bytes 42145152 | solution.py:129
  94.1 17.5 %multiply_subtract_fusion.3 = (f32[4096,256]{1,0:T(8,128)S(1)}, f32[4096,256]{1,0:T(8,128)S(1)}) fusion(f32[4096]{0:T(1024)S(1)} %get-tuple-element.806, f32[4096]{0:T(1024)S(1)} %get-tuple-element.807), kind=kLoop, calls=%fused_computation.13.clone.clone.1 | loop fusion | flops 22020096 | bytes 8421376 | tf_op jit(solution)/shard_map/while/body/eval_jaxpr/sub | solution.py:26
  111.7 2.2 fusion.71
  114.0 1.3 fusion.73
  115.5 0.5 subtract_reduce_fusion.6
  117.3 17.5 %multiply_subtract_fusion.3 = (f32[4096,256]{1,0:T(8,128)S(1)}, f32[4096,256]{1,0:T(8,128)S(1)}) fusion(f32[4096]{0:T(1024)S(1)} %get-tuple-element.806, f32[4096]{0:T(1024)S(1)} %get-tuple-element.807), kind=kLoop, calls=%fused_computation.13.clone.clone.1 | loop fusion | flops 22020096 | bytes 8421376 | tf_op jit(solution)/shard_map/while/body/eval_jaxpr/sub | solution.py:26
  134.8 2.2 fusion.71
  137.1 1.3 fusion.73
  138.6 0.5 subtract_reduce_fusion.6
  139.1 0.5 add_reduce_fusion.6
  140.4 17.5 %multiply_subtract_fusion.3 = (f32[4096,256]{1,0:T(8,128)S(1)}, f32[4096,256]{1,0:T(8,128)S(1)}) fusion(f32[4096]{0:T(1024)S(1)} %get-tuple-element.806, f32[4096]{0:T(1024)S(1)} %get-tuple-element.807), kind=kLoop, calls=%fused_computation.13.clone.clone.1 | loop fusion | flops 22020096 | bytes 8421376 | tf_op jit(solution)/shard_map/while/body/eval_jaxpr/sub | solution.py:26
  157.9 2.2 fusion.71
  160.3 1.3 fusion.73
  161.7 0.5 subtract_reduce_fusion.6
  162.2 0.5 add_reduce_fusion.6
  163.5 17.5 %multiply_subtract_fusion.3 = (f32[4096,256]{1,0:T(8,128)S(1)}, f32[4096,256]{1,0:T(8,128)S(1)}) fusion(f32[4096]{0:T(1024)S(1)} %get-tuple-element.806, f32[4096]{0:T(1024)S(1)} %get-tuple-element.807), kind=kLoop, calls=%fused_computation.13.clone.clone.1 | loop fusion | flops 22020096 | bytes 8421376 | tf_op jit(solution)/shard_map/while/body/eval_jaxpr/sub | solution.py:26
  181.1 2.2 fusion.71
  183.4 1.3 fusion.73
  184.8 0.5 subtract_reduce_fusion.6
  185.3 0.5 add_reduce_fusion.6
  186.7 17.5 %multiply_subtract_fusion.3 = (f32[4096,256]{1,0:T(8,128)S(1)}, f32[4096,256]{1,0:T(8,128)S(1)}) fusion(f32[4096]{0:T(1024)S(1)} %get-tuple-element.806, f32[4096]{0:T(1024)S(1)} %get-tuple-element.807), kind=kLoop, calls=%fused_computation.13.clone.clone.1 | loop fusion | flops 22020096 | bytes 8421376 | tf_op jit(solution)/shard_map/while/body/eval_jaxpr/sub | solution.py:26
  204.2 2.2 fusion.71
  206.5 1.3 fusion.73
  208.0 0.5 subtract_reduce_fusion.6
  209.8 17.5 %multiply_subtract_fusion.3 = (f32[4096,256]{1,0:T(8,128)S(1)}, f32[4096,256]{1,0:T(8,128)S(1)}) fusion(f32[4096]{0:T(1024)S(1)} %get-tuple-element.806, f32[4096]{0:T(1024)S(1)} %get-tuple-element.807), kind=kLoop, calls=%fused_computation.13.clone.clone.1 | loop fusion | flops 22020096 | bytes 8421376 | tf_op jit(solution)/shard_map/while/body/eval_jaxpr/sub | solution.py:26
  227.3 2.2 fusion.71
  229.6 1.3 fusion.73
  231.1 0.5 subtract_reduce_fusion.6
  232.9 17.5 %multiply_subtract_fusion.3 = (f32[4096,256]{1,0:T(8,128)S(1)}, f32[4096,256]{1,0:T(8,128)S(1)}) fusion(f32[4096]{0:T(1024)S(1)} %get-tuple-element.806, f32[4096]{0:T(1024)S(1)} %get-tuple-element.807), kind=kLoop, calls=%fused_computation.13.clone.clone.1 | loop fusion | flops 22020096 | bytes 8421376 | tf_op jit(solution)/shard_map/while/body/eval_jaxpr/sub | solution.py:26
  250.5 2.2 fusion.71
  252.8 1.3 fusion.73
  254.2 0.5 subtract_reduce_fusion.6
  256.0 17.5 %multiply_subtract_fusion.3 = (f32[4096,256]{1,0:T(8,128)S(1)}, f32[4096,256]{1,0:T(8,128)S(1)}) fusion(f32[4096]{0:T(1024)S(1)} %get-tuple-element.806, f32[4096]{0:T(1024)S(1)} %get-tuple-element.807), kind=kLoop, calls=%fused_computation.13.clone.clone.1 | loop fusion | flops 22020096 | bytes 8421376 | tf_op jit(solution)/shard_map/while/body/eval_jaxpr/sub | solution.py:26
  273.6 2.2 fusion.71
  275.9 1.3 fusion.73
  277.4 0.5 subtract_reduce_fusion.6
  279.1 1.0 copy-done.1
  (201 shorter events, 11.3 us)
Async XLA Ops:
  0.0 3.3 %copy-start.6 = (s32[256]{0:T(256)S(1)}, s32[256]{0:T(256)}, u32[]{:S(2)}) copy-start(s32[256]{0:T(256)} %param.8) | copy-start | bytes 3076
  6.8 36.7 %copy-start.5 = (s32[4,2]{0,1:T(2,128)S(1)}, s32[4,2]{0,1:T(2,128)}, u32[]{:S(2)}) copy-start(s32[4,2]{0,1:T(2,128)} %param.11) | copy-start | bytes 100
  6.8 47.3 %copy-start.7 = (s32[16]{0:T(128)S(1)}, s32[16]{0:T(128)}, u32[]{:S(2)}) copy-start(s32[16]{0:T(128)} %param.9) | copy-start | bytes 196
  6.8 47.4 %copy-start.4 = (s32[16,256]{1,0:T(8,128)S(1)}, s32[16,256]{1,0:T(8,128)}, u32[]{:S(2)}) copy-start(s32[16,256]{1,0:T(8,128)} %param.10) | copy-start | bytes 49156
  38.6 52.3 %all-to-all-start.1 = ((bf16[256,16,256]{0,2,1:T(8,128)(2,1)}), bf16[256,16,256]{0,2,1:T(8,128)(2,1)S(1)}, u32[]{:S(2)}, u32[]{:S(2)}) async-start(bf16[256,16,256]{0,2,1:T(8,128)(2,1)} %bitcast.5), calls=%async_computation.1 | async-start | bytes 4194304 | tf_op jit(solution)/shard_map/all_to_all | solution.py:100
  55.0 38.8 %copy-start.2 = (f32[16,8]{1,0:T(8,128)}, f32[16,8]{1,0:T(8,128)S(1)}, u32[]{:S(2)}) copy-start(f32[16,8]{1,0:T(8,128)S(1)} %pad_maximum_fusion) | copy-start | bytes 1540
  55.3 38.6 %copy-start.3 = (f32[1,16,16]{2,1,0:T(8,128)}, f32[1,16,16]{2,1,0:T(8,128)S(1)}, u32[]{:S(2)}) copy-start(f32[1,16,16]{2,1,0:T(8,128)S(1)} %slice.243) | copy-start | bytes 3076
  111.7 2.3 copy-start
  134.8 2.3 copy-start
  157.9 2.3 copy-start
  181.1 2.3 copy-start
  204.2 2.3 copy-start
  227.3 2.3 copy-start
  250.4 2.3 copy-start
  273.6 2.3 copy-start
  279.1 1.0 copy-start.1
where the time goes:
time: 280 us
  other arithmetic  157 us (56%)
  waiting for transfers between devices  34.2 us (12%)
  blocking collectives  31.1 us (11%)
  matrix products  28.3 us (10%)
  local copies, waits for them, and re-layouts  13 us (5%)
  between operations  10.1 us (4%)
  starting transfers between devices  4.91 us (2%)
    sub x8, other arithmetic, rotated_table(): real_part = base_cos * phase_cos - base_sin * phase_sin  140 us
    all_to_all x1, waiting for transfers between devices, per_device(): lax.all_to_all(grouped, 'tm', split_axis=1, concat_axis=0, tiled=True)  34.2 us
    all_to_all x1, blocking collectives, per_device(): lax.all_to_all(margins, 'tm', split_axis=1, concat_axis=0, tiled=True)  31.1 us
    dot_general x16, matrix products, transform(): lax.dot_general(columns, table, (((0,), (0,)), ((), ())), preferred_eleme...  28.3 us
  transfers between devices with their start and end apart: 1, of which 1 were waited for; matrix products, arithmetic and copies ran while one was open for 1% of the time, Pallas kernels for 0%

commit v1 on v0

--- a/solution.py
+++ b/solution.py
@@ -1,3 +1,4 @@
+import functools
 import math
 import jax
 import jax.numpy as jnp
@@ -7,6 +8,24 @@
 ROWS = 16
 BAND = 256
 REACH = 4
+
+
+def read_rates_here(raw, a_name):
+    res, main = (jax.lax.axis_size(a_name), jax.lax.axis_index(a_name))
+    small = raw.shape[1] // res
+    known = jnp.roll(raw, -main * small, 1)
+    nth = 1
+    stack_in = [lax.slice_in_dim(known, 0, small, axis=1)]
+    while nth < res:
+        state_next = lax.slice_in_dim(known, nth * small, (nth + 1) * small, axis=1)
+        stack_in.append(
+            jax.lax.ppermute(state_next, a_name, [(p, (p + nth) % res) for p in range(res)])
+        )
+        nth += 1
+    return jnp.roll(jnp.concatenate(stack_in[::-1], 0), (main + 1) * stack_in[0].shape[0], 0)
+
+
+_store_wires = functools.partial(read_rates_here, a_name="tm")
 
 
 def base_angles(frames_len, band_width):
@@ -98,7 +117,7 @@
     )
     tile_frames, margin_frames = (
         lax.all_to_all(grouped, "tm", split_axis=1, concat_axis=0, tiled=True),
-        lax.all_to_all(margins, "tm", split_axis=1, concat_axis=0, tiled=True),
+        _store_wires(margins),
     )
     margin_frames = margin_frames.reshape(-1, ROWS * 2 * REACH)
     margin_valid = jnp.concatenate(

time: 280 us -> 283 us (1.011); the launches traced: 280 us -> 278 us
  starting transfers between devices: 4.91 us -> 47.2 us
  blocking collectives: 31.1 us -> 0 us
  waiting for transfers between devices: 34.2 us -> 19.2 us
  matrix products: 28.3 us -> 17.6 us
  local copies, waits for them, and re-layouts: 13 us -> 19.5 us
  other arithmetic: 157 us -> 162 us
    ppermute x0 -> x15, starting transfers between devices: none -> 40 us  [read_rates_here(): jax.lax.ppermute(state_next, a_name, [(p, (p + nth) % res) for p in range...]
    all_to_all x1, waiting for transfers between devices: 34.2 us -> 0.01 us  [per_device(): lax.all_to_all(grouped, 'tm', split_axis=1, concat_axis=0, tiled=True)]
    all_to_all x1 -> x0, blocking collectives: 31.1 us -> none  [per_device(): lax.all_to_all(margins, 'tm', split_axis=1, concat_axis=0, tiled=True)]
    ppermute x0 -> x15, waiting for transfers between devices: none -> 19.1 us  [read_rates_here(): jax.lax.ppermute(state_next, a_name, [(p, (p + nth) % res) for p in range...]
    dot_general x16, matrix products: 28.3 us -> 17.6 us  [transform(): lax.dot_general(columns, table, (((0,), (0,)), ((), ())), preferred_eleme...]
    while x16 -> x32, local copies, waits for them, and re-layouts: 0.03 us -> 5.19 us
    dynamic_update_slice x8, other arithmetic: 0.7 us -> 5.76 us  [one_band(): lax.dynamic_update_slice(result, band_cross, (jnp.int32(0), jnp.int32(0),...]
  transfers between devices with their start and end apart: 1 -> 16, of which waited for: 1 -> 2; matrix products, arithmetic and copies ran while one was open for 1% -> 1% of each run, Pallas kernels for 0% -> 0%
where the time goes in v1:
time: 283 us; the launch traced here: 278 us
  other arithmetic  162 us (57%)
  starting transfers between devices  47.2 us (17%)
  local copies, waits for them, and re-layouts  19.5 us (7%)
  waiting for transfers between devices  19.2 us (7%)
  matrix products  17.6 us (6%)
  between operations  10.7 us (4%)
    sub x8, other arithmetic, rotated_table(): real_part = base_cos * phase_cos - base_sin * phase_sin  140 us
    ppermute x15, starting transfers between devices, read_rates_here(): jax.lax.ppermute(state_next, a_name, [(p, (p + nth) % res) for p in range...  40 us
    ppermute x15, waiting for transfers between devices, read_rates_here(): jax.lax.ppermute(state_next, a_name, [(p, (p + nth) % res) for p in range...  19.1 us
    dot_general x16, matrix products, transform(): lax.dot_general(columns, table, (((0,), (0,)), ((), ())), preferred_eleme...  17.6 us
    all_to_all x1, starting transfers between devices, per_device(): lax.all_to_all(grouped, 'tm', split_axis=1, concat_axis=0, tiled=True)  7.16 us
    dynamic_update_slice x8, other arithmetic, one_band(): lax.dynamic_update_slice(result, band_cross, (jnp.int32(0), jnp.int32(0),...  5.76 us
  transfers between devices with their start and end apart: 16, of which 2 were waited for; matrix products, arithmetic and copies ran while one was open for 1% of the time, Pallas kernels for 0%

profile of v1, /device:TPU:11, one launch (start us, length us, event | category | flops | bytes accessed | tf_op | source)
XLA Modules:
  0.0 277.5 jit_solution(4326087584479211529)
XLA Ops:
  0.0 3.3 %copy.13 = bf16[256,4096]{0,1:T(8,128)(2,1)S(1)} copy(bf16[256,4096]{1,0:T(8,128)(2,1)} %param.7) | data formatting | bytes 4194304 | tf_op args[0]
  3.3 1.5 broadcast_multiply_fusion
  4.8 2.0 fusion.45
  7.9 0.9 fusion.46
  9.7 1.3 collective-permute-start.2
  11.0 3.3 %collective-permute-start.3 = (bf16[256,1,128]{0,2,1:T(8,128)(2,1)}, bf16[256,1,128]{0,2,1:T(8,128)(2,1)S(1)}, u32[]{:S(2)}, u32[]{:S(2)}) collective-permute-start(bf16[256,1,128]{0,2,1:T(8,128)(2,1)} %get-tuple-element.592), channel_id=1, source_target_pairs={{0,12},{1,13},{2,14},{3,15},{4,0},{5,1},{6,2},{7,3},{8,4},{9,5},{1... | collective-permute-start | bytes 196616 | tf_op jit(solution)/shard_map/ppermute | solution.py:22
  14.5 7.2 %all-to-all-start = ((bf16[256,16,256]{0,2,1:T(8,128)(2,1)}), bf16[256,16,256]{0,2,1:T(8,128)(2,1)S(1)}, u32[]{:S(2)}, u32[]{:S(2)}) async-start(bf16[256,16,256]{0,2,1:T(8,128)(2,1)} %bitcast.3), calls=%async_computation | async-start | bytes 4194304 | tf_op jit(solution)/shard_map/all_to_all | solution.py:119
  34.0 3.8 %collective-permute-start.6 = (bf16[256,1,128]{0,2,1:T(8,128)(2,1)}, bf16[256,1,128]{0,2,1:T(8,128)(2,1)S(1)}, u32[]{:S(2)}, u32[]{:S(2)}) collective-permute-start(bf16[256,1,128]{0,2,1:T(8,128)(2,1)} %get-tuple-element.589), channel_id=1, source_target_pairs={{0,9},{1,10},{2,11},{3,12},{4,13},{5,14},{6,15},{7,0},{8,1},{9,2},... | collective-permute-start | bytes 196616 | tf_op jit(solution)/shard_map/ppermute | solution.py:22
  38.2 1.2 collective-permute-start.8
  39.4 3.0 %collective-permute-start.9 = (bf16[256,1,128]{0,2,1:T(8,128)(2,1)}, bf16[256,1,128]{0,2,1:T(8,128)(2,1)S(1)}, u32[]{:S(2)}, u32[]{:S(2)}) collective-permute-start(bf16[256,1,128]{0,2,1:T(8,128)(2,1)} %get-tuple-element.586), channel_id=1, source_target_pairs={{0,6},{1,7},{2,8},{3,9},{4,10},{5,11},{6,12},{7,13},{8,14},{9,15},... | collective-permute-start | bytes 196616 | tf_op jit(solution)/shard_map/ppermute | solution.py:22
  42.5 17.4 %collective-permute-done.5 = bf16[256,1,128]{0,2,1:T(8,128)(2,1)S(1)} collective-permute-done((bf16[256,1,128]{0,2,1:T(8,128)(2,1)}, bf16[256,1,128]{0,2,1:T(8,128)(2,1)S(1)}, u32[]{:S(2)}, u32[]{:S(2)}) %collective-permute-start.5) | collective-permute-done | bytes 65568 | tf_op jit(solution)/shard_map/ppermute | solution.py:22
  59.8 3.0 %collective-permute-start.10 = (bf16[256,1,128]{0,2,1:T(8,128)(2,1)}, bf16[256,1,128]{0,2,1:T(8,128)(2,1)S(1)}, u32[]{:S(2)}, u32[]{:S(2)}) collective-permute-start(bf16[256,1,128]{0,2,1:T(8,128)(2,1)} %get-tuple-element.585), channel_id=1, source_target_pairs={{0,5},{1,6},{2,7},{3,8},{4,9},{5,10},{6,11},{7,12},{8,13},{9,14},{... | collective-permute-start | bytes 196616 | tf_op jit(solution)/shard_map/ppermute | solution.py:22
  62.9 13.0 %collective-permute-start.11 = (bf16[256,1,128]{0,2,1:T(8,128)(2,1)}, bf16[256,1,128]{0,2,1:T(8,128)(2,1)S(1)}, u32[]{:S(2)}, u32[]{:S(2)}) collective-permute-start(bf16[256,1,128]{0,2,1:T(8,128)(2,1)} %get-tuple-element.584), channel_id=1, source_target_pairs={{0,4},{1,5},{2,6},{3,7},{4,8},{5,9},{6,10},{7,11},{8,12},{9,13},{1... | collective-permute-start | bytes 196616 | tf_op jit(solution)/shard_map/ppermute | solution.py:22
  75.9 6.2 %collective-permute-start.12 = (bf16[256,1,128]{0,2,1:T(8,128)(2,1)}, bf16[256,1,128]{0,2,1:T(8,128)(2,1)S(1)}, u32[]{:S(2)}, u32[]{:S(2)}) collective-permute-start(bf16[256,1,128]{0,2,1:T(8,128)(2,1)} %get-tuple-element.583), channel_id=1, source_target_pairs={{0,3},{1,4},{2,5},{3,6},{4,7},{5,8},{6,9},{7,10},{8,11},{9,12},{10... | collective-permute-start | bytes 196616 | tf_op jit(solution)/shard_map/ppermute | solution.py:22
  82.1 1.8 collective-permute-start.13
  84.0 1.8 collective-permute-start.14
  85.9 1.7 collective-permute-done.14
  87.9 1.3 copy.14
  89.3 2.4 copy.15
  91.6 1.5 broadcast_in_dim.14
  93.1 184.4 %while.19 = (s32[]{:T(128)}, f32[16,4,2,2048]{3,2,1,0:T(2,128)}, bf16[4096,128]{1,0:T(8,128)(2,1)}, f32[16,8]{1,0:T(8,128)}, bf16[4096,256]{1,0:T(8,128)(2,1)}, ...) while((s32[]{:T(128)}, f32[16,4,2,2048]{3,2,1,0:T(2,128)}, ...), condition=%wide.wide.region_14.15_spmd.clone.clone, body=%wide.wide.region_1.14_spmd.clone.clone.sunk | while | flops 1649076224 | bytes 46339488 | solution.py:148
  93.2 17.5 %multiply_subtract_fusion.3 = (f32[4096,256]{1,0:T(8,128)S(1)}, f32[4096,256]{1,0:T(8,128)S(1)}) fusion(f32[4096]{0:T(1024)S(1)} %get-tuple-element.821, f32[4096]{0:T(1024)S(1)} %get-tuple-element.822), kind=kLoop, calls=%fused_computation.13.clone.clone.1 | loop fusion | flops 22020096 | bytes 8421376 | tf_op jit(solution)/shard_map/while/body/eval_jaxpr/sub | solution.py:45
  110.8 0.9 fusion.73
  112.4 1.3 fusion.75
  115.5 0.7 maximum_dynamic-update-slice_fusion.3
  116.3 17.5 %multiply_subtract_fusion.3 = (f32[4096,256]{1,0:T(8,128)S(1)}, f32[4096,256]{1,0:T(8,128)S(1)}) fusion(f32[4096]{0:T(1024)S(1)} %get-tuple-element.821, f32[4096]{0:T(1024)S(1)} %get-tuple-element.822), kind=kLoop, calls=%fused_computation.13.clone.clone.1 | loop fusion | flops 22020096 | bytes 8421376 | tf_op jit(solution)/shard_map/while/body/eval_jaxpr/sub | solution.py:45
  133.8 0.9 fusion.73
  135.4 1.3 fusion.75
  138.5 0.7 maximum_dynamic-update-slice_fusion.3
  139.3 17.5 %multiply_subtract_fusion.3 = (f32[4096,256]{1,0:T(8,128)S(1)}, f32[4096,256]{1,0:T(8,128)S(1)}) fusion(f32[4096]{0:T(1024)S(1)} %get-tuple-element.821, f32[4096]{0:T(1024)S(1)} %get-tuple-element.822), kind=kLoop, calls=%fused_computation.13.clone.clone.1 | loop fusion | flops 22020096 | bytes 8421376 | tf_op jit(solution)/shard_map/while/body/eval_jaxpr/sub | solution.py:45
  156.9 0.9 fusion.73
  158.5 1.3 fusion.75
  161.6 0.7 maximum_dynamic-update-slice_fusion.3
  162.4 17.5 %multiply_subtract_fusion.3 = (f32[4096,256]{1,0:T(8,128)S(1)}, f32[4096,256]{1,0:T(8,128)S(1)}) fusion(f32[4096]{0:T(1024)S(1)} %get-tuple-element.821, f32[4096]{0:T(1024)S(1)} %get-tuple-element.822), kind=kLoop, calls=%fused_computation.13.clone.clone.1 | loop fusion | flops 22020096 | bytes 8421376 | tf_op jit(solution)/shard_map/while/body/eval_jaxpr/sub | solution.py:45
  179.9 0.9 fusion.73
  181.5 1.3 fusion.75
  185.4 17.5 %multiply_subtract_fusion.3 = (f32[4096,256]{1,0:T(8,128)S(1)}, f32[4096,256]{1,0:T(8,128)S(1)}) fusion(f32[4096]{0:T(1024)S(1)} %get-tuple-element.821, f32[4096]{0:T(1024)S(1)} %get-tuple-element.822), kind=kLoop, calls=%fused_computation.13.clone.clone.1 | loop fusion | flops 22020096 | bytes 8421376 | tf_op jit(solution)/shard_map/while/body/eval_jaxpr/sub | solution.py:45
  203.0 0.9 fusion.73
  204.6 1.3 fusion.75
  208.5 17.5 %multiply_subtract_fusion.3 = (f32[4096,256]{1,0:T(8,128)S(1)}, f32[4096,256]{1,0:T(8,128)S(1)}) fusion(f32[4096]{0:T(1024)S(1)} %get-tuple-element.821, f32[4096]{0:T(1024)S(1)} %get-tuple-element.822), kind=kLoop, calls=%fused_computation.13.clone.clone.1 | loop fusion | flops 22020096 | bytes 8421376 | tf_op jit(solution)/shard_map/while/body/eval_jaxpr/sub | solution.py:45
  226.0 0.9 fusion.73
  227.6 1.3 fusion.75
  231.5 17.5 %multiply_subtract_fusion.3 = (f32[4096,256]{1,0:T(8,128)S(1)}, f32[4096,256]{1,0:T(8,128)S(1)}) fusion(f32[4096]{0:T(1024)S(1)} %get-tuple-element.821, f32[4096]{0:T(1024)S(1)} %get-tuple-element.822), kind=kLoop, calls=%fused_computation.13.clone.clone.1 | loop fusion | flops 22020096 | bytes 8421376 | tf_op jit(solution)/shard_map/while/body/eval_jaxpr/sub | solution.py:45
  249.1 0.9 fusion.73
  250.6 1.3 fusion.75
  254.6 17.5 %multiply_subtract_fusion.3 = (f32[4096,256]{1,0:T(8,128)S(1)}, f32[4096,256]{1,0:T(8,128)S(1)}) fusion(f32[4096]{0:T(1024)S(1)} %get-tuple-element.821, f32[4096]{0:T(1024)S(1)} %get-tuple-element.822), kind=kLoop, calls=%fused_computation.13.clone.clone.1 | loop fusion | flops 22020096 | bytes 8421376 | tf_op jit(solution)/shard_map/while/body/eval_jaxpr/sub | solution.py:45
  272.1 0.9 fusion.73
  273.7 1.3 fusion.75
  (279 shorter events, 27.9 us)
Async XLA Ops:
  0.0 3.3 %copy-start.6 = (s32[256]{0:T(256)S(1)}, s32[256]{0:T(256)}, u32[]{:S(2)}) copy-start(s32[256]{0:T(256)} %param.8) | copy-start | bytes 3076
  8.8 25.1 %collective-permute-start = (bf16[256,1,128]{0,2,1:T(8,128)(2,1)}, bf16[256,1,128]{0,2,1:T(8,128)(2,1)S(1)}, u32[]{:S(2)}, u32[]{:S(2)}) collective-permute-start(bf16[256,1,128]{0,2,1:T(8,128)(2,1)} %get-tuple-element.595), channel_id=1, source_target_pairs={{0,15},{1,0},{2,1},{3,2},{4,3},{5,4},{6,5},{7,6},{8,7},{9,8},{10,9... | collective-permute-start | bytes 196616 | tf_op jit(solution)/shard_map/ppermute | solution.py:22
  9.5 24.6 %collective-permute-start.1 = (bf16[256,1,128]{0,2,1:T(8,128)(2,1)}, bf16[256,1,128]{0,2,1:T(8,128)(2,1)S(1)}, u32[]{:S(2)}, u32[]{:S(2)}) collective-permute-start(bf16[256,1,128]{0,2,1:T(8,128)(2,1)} %get-tuple-element.594), channel_id=1, source_target_pairs={{0,14},{1,15},{2,0},{3,1},{4,2},{5,3},{6,4},{7,5},{8,6},{9,7},{10,... | collective-permute-start | bytes 196616 | tf_op jit(solution)/shard_map/ppermute | solution.py:22
  9.7 28.1 %collective-permute-start.2 = (bf16[256,1,128]{0,2,1:T(8,128)(2,1)}, bf16[256,1,128]{0,2,1:T(8,128)(2,1)S(1)}, u32[]{:S(2)}, u32[]{:S(2)}) collective-permute-start(bf16[256,1,128]{0,2,1:T(8,128)(2,1)} %get-tuple-element.593), channel_id=1, source_target_pairs={{0,13},{1,14},{2,15},{3,0},{4,1},{5,2},{6,3},{7,4},{8,5},{9,6},{10... | collective-permute-start | bytes 196616 | tf_op jit(solution)/shard_map/ppermute | solution.py:22
  11.0 27.1 %collective-permute-start.3 = (bf16[256,1,128]{0,2,1:T(8,128)(2,1)}, bf16[256,1,128]{0,2,1:T(8,128)(2,1)S(1)}, u32[]{:S(2)}, u32[]{:S(2)}) collective-permute-start(bf16[256,1,128]{0,2,1:T(8,128)(2,1)} %get-tuple-element.592), channel_id=1, source_target_pairs={{0,12},{1,13},{2,14},{3,15},{4,0},{5,1},{6,2},{7,3},{8,4},{9,5},{1... | collective-permute-start | bytes 196616 | tf_op jit(solution)/shard_map/ppermute | solution.py:22
  14.3 25.1 %collective-permute-start.4 = (bf16[256,1,128]{0,2,1:T(8,128)(2,1)}, bf16[256,1,128]{0,2,1:T(8,128)(2,1)S(1)}, u32[]{:S(2)}, u32[]{:S(2)}) collective-permute-start(bf16[256,1,128]{0,2,1:T(8,128)(2,1)} %get-tuple-element.591), channel_id=1, source_target_pairs={{0,11},{1,12},{2,13},{3,14},{4,15},{5,0},{6,1},{7,2},{8,3},{9,4},{... | collective-permute-start | bytes 196616 | tf_op jit(solution)/shard_map/ppermute | solution.py:22
  14.5 7.2 %copy-start.5 = (s32[4,2]{0,1:T(2,128)S(1)}, s32[4,2]{0,1:T(2,128)}, u32[]{:S(2)}) copy-start(s32[4,2]{0,1:T(2,128)} %param.11) | copy-start | bytes 100
  14.5 18.2 %copy-start.7 = (s32[16]{0:T(128)S(1)}, s32[16]{0:T(128)}, u32[]{:S(2)}) copy-start(s32[16]{0:T(128)} %param.9) | copy-start | bytes 196
  14.5 18.3 %copy-start.4 = (s32[16,256]{1,0:T(8,128)S(1)}, s32[16,256]{1,0:T(8,128)}, u32[]{:S(2)}) copy-start(s32[16,256]{1,0:T(8,128)} %param.10) | copy-start | bytes 49156
  14.5 74.8 %all-to-all-start = ((bf16[256,16,256]{0,2,1:T(8,128)(2,1)}), bf16[256,16,256]{0,2,1:T(8,128)(2,1)S(1)}, u32[]{:S(2)}, u32[]{:S(2)}) async-start(bf16[256,16,256]{0,2,1:T(8,128)(2,1)} %bitcast.3), calls=%async_computation | async-start | bytes 4194304 | tf_op jit(solution)/shard_map/all_to_all | solution.py:119
  33.5 54.3 %copy-start.2 = (f32[16,8]{1,0:T(8,128)}, f32[16,8]{1,0:T(8,128)S(1)}, u32[]{:S(2)}) copy-start(f32[16,8]{1,0:T(8,128)S(1)} %pad_maximum_fusion) | copy-start | bytes 1540
  33.7 54.1 %copy-start.3 = (f32[1,16,16]{2,1,0:T(8,128)}, f32[1,16,16]{2,1,0:T(8,128)S(1)}, u32[]{:S(2)}) copy-start(f32[1,16,16]{2,1,0:T(8,128)S(1)} %slice.307) | copy-start | bytes 3076
  33.9 25.9 %collective-permute-start.5 = (bf16[256,1,128]{0,2,1:T(8,128)(2,1)}, bf16[256,1,128]{0,2,1:T(8,128)(2,1)S(1)}, u32[]{:S(2)}, u32[]{:S(2)}) collective-permute-start(bf16[256,1,128]{0,2,1:T(8,128)(2,1)} %get-tuple-element.590), channel_id=1, source_target_pairs={{0,10},{1,11},{2,12},{3,13},{4,14},{5,15},{6,0},{7,1},{8,2},{9,3},... | collective-permute-start | bytes 196616 | tf_op jit(solution)/shard_map/ppermute | solution.py:22
  34.0 28.8 %collective-permute-start.6 = (bf16[256,1,128]{0,2,1:T(8,128)(2,1)}, bf16[256,1,128]{0,2,1:T(8,128)(2,1)S(1)}, u32[]{:S(2)}, u32[]{:S(2)}) collective-permute-start(bf16[256,1,128]{0,2,1:T(8,128)(2,1)} %get-tuple-element.589), channel_id=1, source_target_pairs={{0,9},{1,10},{2,11},{3,12},{4,13},{5,14},{6,15},{7,0},{8,1},{9,2},... | collective-permute-start | bytes 196616 | tf_op jit(solution)/shard_map/ppermute | solution.py:22
  37.8 38.1 %collective-permute-start.7 = (bf16[256,1,128]{0,2,1:T(8,128)(2,1)}, bf16[256,1,128]{0,2,1:T(8,128)(2,1)S(1)}, u32[]{:S(2)}, u32[]{:S(2)}) collective-permute-start(bf16[256,1,128]{0,2,1:T(8,128)(2,1)} %get-tuple-element.588), channel_id=1, source_target_pairs={{0,8},{1,9},{2,10},{3,11},{4,12},{5,13},{6,14},{7,15},{8,0},{9,1},... | collective-permute-start | bytes 196616 | tf_op jit(solution)/shard_map/ppermute | solution.py:22
  38.2 43.9 %collective-permute-start.8 = (bf16[256,1,128]{0,2,1:T(8,128)(2,1)}, bf16[256,1,128]{0,2,1:T(8,128)(2,1)S(1)}, u32[]{:S(2)}, u32[]{:S(2)}) collective-permute-start(bf16[256,1,128]{0,2,1:T(8,128)(2,1)} %get-tuple-element.587), channel_id=1, source_target_pairs={{0,7},{1,8},{2,9},{3,10},{4,11},{5,12},{6,13},{7,14},{8,15},{9,0},... | collective-permute-start | bytes 196616 | tf_op jit(solution)/shard_map/ppermute | solution.py:22
  39.4 44.5 %collective-permute-start.9 = (bf16[256,1,128]{0,2,1:T(8,128)(2,1)}, bf16[256,1,128]{0,2,1:T(8,128)(2,1)S(1)}, u32[]{:S(2)}, u32[]{:S(2)}) collective-permute-start(bf16[256,1,128]{0,2,1:T(8,128)(2,1)} %get-tuple-element.586), channel_id=1, source_target_pairs={{0,6},{1,7},{2,8},{3,9},{4,10},{5,11},{6,12},{7,13},{8,14},{9,15},... | collective-permute-start | bytes 196616 | tf_op jit(solution)/shard_map/ppermute | solution.py:22
  59.8 25.9 %collective-permute-start.10 = (bf16[256,1,128]{0,2,1:T(8,128)(2,1)}, bf16[256,1,128]{0,2,1:T(8,128)(2,1)S(1)}, u32[]{:S(2)}, u32[]{:S(2)}) collective-permute-start(bf16[256,1,128]{0,2,1:T(8,128)(2,1)} %get-tuple-element.585), channel_id=1, source_target_pairs={{0,5},{1,6},{2,7},{3,8},{4,9},{5,10},{6,11},{7,12},{8,13},{9,14},{... | collective-permute-start | bytes 196616 | tf_op jit(solution)/shard_map/ppermute | solution.py:22
  62.9 22.9 %collective-permute-start.11 = (bf16[256,1,128]{0,2,1:T(8,128)(2,1)}, bf16[256,1,128]{0,2,1:T(8,128)(2,1)S(1)}, u32[]{:S(2)}, u32[]{:S(2)}) collective-permute-start(bf16[256,1,128]{0,2,1:T(8,128)(2,1)} %get-tuple-element.584), channel_id=1, source_target_pairs={{0,4},{1,5},{2,6},{3,7},{4,8},{5,9},{6,10},{7,11},{8,12},{9,13},{1... | collective-permute-start | bytes 196616 | tf_op jit(solution)/shard_map/ppermute | solution.py:22
  75.9 9.9 %collective-permute-start.12 = (bf16[256,1,128]{0,2,1:T(8,128)(2,1)}, bf16[256,1,128]{0,2,1:T(8,128)(2,1)S(1)}, u32[]{:S(2)}, u32[]{:S(2)}) collective-permute-start(bf16[256,1,128]{0,2,1:T(8,128)(2,1)} %get-tuple-element.583), channel_id=1, source_target_pairs={{0,3},{1,4},{2,5},{3,6},{4,7},{5,8},{6,9},{7,10},{8,11},{9,12},{10... | collective-permute-start | bytes 196616 | tf_op jit(solution)/shard_map/ppermute | solution.py:22
  82.1 3.7 %collective-permute-start.13 = (bf16[256,1,128]{0,2,1:T(8,128)(2,1)}, bf16[256,1,128]{0,2,1:T(8,128)(2,1)S(1)}, u32[]{:S(2)}, u32[]{:S(2)}) collective-permute-start(bf16[256,1,128]{0,2,1:T(8,128)(2,1)} %get-tuple-element.582), channel_id=1, source_target_pairs={{0,2},{1,3},{2,4},{3,5},{4,6},{5,7},{6,8},{7,9},{8,10},{9,11},{10,... | collective-permute-start | bytes 196616 | tf_op jit(solution)/shard_map/ppermute | solution.py:22
  84.0 3.6 %collective-permute-start.14 = (bf16[256,1,128]{0,2,1:T(8,128)(2,1)}, bf16[256,1,128]{0,2,1:T(8,128)(2,1)S(1)}, u32[]{:S(2)}, u32[]{:S(2)}) collective-permute-start(bf16[256,1,128]{0,2,1:T(8,128)(2,1)} %get-tuple-element.581), channel_id=1, source_target_pairs={{0,1},{1,2},{2,3},{3,4},{4,5},{5,6},{6,7},{7,8},{8,9},{9,10},{10,1... | collective-permute-start | bytes 196616 | tf_op jit(solution)/shard_map/ppermute | solution.py:22
  93.2 17.5 %copy-start.1 = (bf16[4096,128]{1,0:T(8,128)(2,1)S(1)}, bf16[4096,128]{1,0:T(8,128)(2,1)}, u32[]{:S(2)}) copy-start(bf16[4096,128]{1,0:T(8,128)(2,1)} %get-tuple-element.891) | copy-start | bytes 3145732 | tf_op jit(solution)/shard_map/while
  110.8 1.6 copy-start
  116.3 17.5 %copy-start.1 = (bf16[4096,128]{1,0:T(8,128)(2,1)S(1)}, bf16[4096,128]{1,0:T(8,128)(2,1)}, u32[]{:S(2)}) copy-start(bf16[4096,128]{1,0:T(8,128)(2,1)} %get-tuple-element.891) | copy-start | bytes 3145732 | tf_op jit(solution)/shard_map/while
  133.8 1.6 copy-start
  139.3 17.5 %copy-start.1 = (bf16[4096,128]{1,0:T(8,128)(2,1)S(1)}, bf16[4096,128]{1,0:T(8,128)(2,1)}, u32[]{:S(2)}) copy-start(bf16[4096,128]{1,0:T(8,128)(2,1)} %get-tuple-element.891) | copy-start | bytes 3145732 | tf_op jit(solution)/shard_map/while
  156.9 1.6 copy-start
  162.4 17.5 %copy-start.1 = (bf16[4096,128]{1,0:T(8,128)(2,1)S(1)}, bf16[4096,128]{1,0:T(8,128)(2,1)}, u32[]{:S(2)}) copy-start(bf16[4096,128]{1,0:T(8,128)(2,1)} %get-tuple-element.891) | copy-start | bytes 3145732 | tf_op jit(solution)/shard_map/while
  179.9 1.6 copy-start
  185.4 17.5 %copy-start.1 = (bf16[4096,128]{1,0:T(8,128)(2,1)S(1)}, bf16[4096,128]{1,0:T(8,128)(2,1)}, u32[]{:S(2)}) copy-start(bf16[4096,128]{1,0:T(8,128)(2,1)} %get-tuple-element.891) | copy-start | bytes 3145732 | tf_op jit(solution)/shard_map/while
  203.0 1.6 copy-start
  208.4 17.5 %copy-start.1 = (bf16[4096,128]{1,0:T(8,128)(2,1)S(1)}, bf16[4096,128]{1,0:T(8,128)(2,1)}, u32[]{:S(2)}) copy-start(bf16[4096,128]{1,0:T(8,128)(2,1)} %get-tuple-element.891) | copy-start | bytes 3145732 | tf_op jit(solution)/shard_map/while
  226.0 1.6 copy-start
  231.5 17.5 %copy-start.1 = (bf16[4096,128]{1,0:T(8,128)(2,1)S(1)}, bf16[4096,128]{1,0:T(8,128)(2,1)}, u32[]{:S(2)}) copy-start(bf16[4096,128]{1,0:T(8,128)(2,1)} %get-tuple-element.891) | copy-start | bytes 3145732 | tf_op jit(solution)/shard_map/while
  249.1 1.6 copy-start
  254.5 17.5 %copy-start.1 = (bf16[4096,128]{1,0:T(8,128)(2,1)S(1)}, bf16[4096,128]{1,0:T(8,128)(2,1)}, u32[]{:S(2)}) copy-start(bf16[4096,128]{1,0:T(8,128)(2,1)} %get-tuple-element.891) | copy-start | bytes 3145732 | tf_op jit(solution)/shard_map/while
  272.1 1.6 copy-start
